TPU v7x, 256 devices: a whole 4x4x8 slice. The times are simulated.
256 devices in a mesh: ex: 32 (over z, y_lo, core), tok: 8 (over y_hi, x).
Axes of the slice: x: 4, y: 4 (y_hi: 2, y_lo: 2; y = y_hi * 2 + y_lo), z: 8, core: 2. Of those that a mesh axis runs over, the one named last changes fastest.
Arguments:
- activations: bfloat16 [8192, 32, 4096], P(('ex', 'tok')), may hold values from -6 to 6
- out_grads: bfloat16 [8192, 32, 2, 1024], P(('ex', 'tok')), may hold values from -6 to 6
- block_len: int32 [8192], P(('ex', 'tok')), may hold values from 1 to 32
- block_dest: int32 [8192, 1], P(('ex', 'tok')), may hold values from 0 to 31; in each aligned block of 32 rows (0 to 31, 32 to 63, ...) at most 2 rows name the same one
- block_slot: int32 [8192], P(('ex', 'tok')), may hold values from 0 to 3
- in_proj: bfloat16 [4096, 128], replicated, may hold values from -0.09375 to 0.09375
- out_proj: bfloat16 [2, 1024, 64], replicated, may hold values from -0.1875 to 0.1875
- query_grads: float32 [64, 8192], P('ex'), may hold values from -6 to 6
- precond: float32 [2, 2, 64, 64], replicated, may hold values from -2 to 2, as said below
Outputs:
- scores: float32 [64, 128], P('tok', 'ex')
Inputs may be any that keep to these rules, and one draw needn't show every extreme that they name: `block_dest`: among the 32 blocks of one device no index of ex is named more than 2 times, a bound that some device reaches; every index of ex is named by some block of the whole array. `precond`: entries of order one or less.
All inputs are finite; a program needn't handle non-finite values.
Results may differ from a plain program's by a relative error of at most 0.0003.
Values sent between devices are 32-bit elements; how exact they have to be, the bound alone decides.
A program may use at most 64 MiB of HBM per device.

v0:
```python
import jax
import jax.numpy as jnp
from jax import lax
from jax.sharding import PartitionSpec as P

R = 64
BLK = 32
EX_DEV = 4
F = 8192
highest = lax.Precision.HIGHEST


def on_device(
    activations,
    out_grads,
    block_len,
    block_dest,
    block_slot,
    in_proj,
    out_proj,
    query_grads,
    precond,
):
    block_count = activations.shape[0]
    block_size = activations.shape[1]
    ex_count = lax.axis_size("ex")
    proj_in = jnp.dot(
        activations.reshape(block_count * block_size, -1),
        in_proj,
        preferred_element_type=jnp.float32,
    )
    proj_in = proj_in.reshape(block_count, block_size, 2, R)
    proj_out = jnp.einsum("btlk,lkr->btlr", out_grads, out_proj, preferred_element_type=jnp.float32)
    position = lax.broadcasted_iota(jnp.int32, (block_count, block_size), 1)
    live_mask = (position < block_len[:, None]).astype(jnp.float32)
    proj_out = proj_out * live_mask[:, :, None, None]
    partial_value = jnp.einsum("btlo,btli->bloi", proj_out, proj_in, precision=highest).reshape(
        block_count, F
    )
    target = block_dest[:, 0]
    example = target * EX_DEV + block_slot
    by_example = (
        example[:, None] == jnp.arange(ex_count * EX_DEV, dtype=jnp.int32)[None, :]
    ).astype(jnp.float32)
    table = jnp.dot(by_example.T, partial_value, precision=highest)
    features = lax.psum_scatter(table, "ex", scatter_dimension=0, tiled=True)
    query_count = query_grads.shape[0]
    queries = query_grads.reshape(query_count, 2, R, R)
    left_side = jnp.einsum("lab,qlbc->qlac", precond[:, 0], queries, precision=highest)
    conditioned = jnp.einsum("qlac,lcd->qlad", left_side, precond[:, 1], precision=highest).reshape(
        query_count, F
    )
    score_terms = jnp.dot(
        lax.all_gather(conditioned, "ex", axis=0, tiled=True), features.T, precision=highest
    ) * (1.0 / (R * BLK))
    return lax.psum_scatter(score_terms, "tok", scatter_dimension=0, tiled=True)


def solution(mesh):
    placed = (
        P(("ex", "tok"), None, None),
        P(("ex", "tok"), None, None, None),
        P(("ex", "tok")),
        P(("ex", "tok"), None),
        P(("ex", "tok")),
        P(),
        P(),
        P("ex", None),
        P(),
    )
    return jax.shard_map(
        on_device, mesh=mesh, in_specs=placed, out_specs=P("tok", "ex"), check_vma=False
    )
```

profile of v0, /device:TPU:0, one launch (start us, length us, event | category | flops | bytes accessed | tf_op | source)
XLA Modules:
  0.0 353.2 jit_solution(176973868079033243)
XLA Ops:
  6.5 0.0 copy-start
  6.5 0.0 all-gather.3.cloned.1.call-start
  6.5 1.0 reshape.37
  7.6 1.2 convolution_bitcast_fusion.1
  8.8 1.2 convolution_bitcast_fusion
  10.0 0.7 reshape.40
  10.8 0.0 all-gather.3.cloned.1.call-update
  10.8 0.0 all-reduce.4.cloned.1.call-start
  10.9 1.5 copy.20
  12.3 0.7 fusion.18
  13.1 0.0 copy-done
  13.1 3.4 fusion.7
  16.5 4.9 %fusion = f32[32,32,2,64]{3,1,2,0:T(8,128)S(1)} fusion(bf16[2,64,4096,1]{2,1,0,3:T(8,128)(2,1)S(1)} %bitcast.51, bf16[32,32,4096]{2,1,0:T(8,128)(2,1)} %param.9), kind=kOutput, calls=%fused_computation | convolution fusion | flops 1073741824 | bytes 9961472 | tf_op jit(solution)/shard_map/dot_general | solution.py:27
  21.4 0.0 copy-start.1
  21.4 0.0 copy-start.2
  21.4 3.7 %fusion.21 = f32[32,2,64,64]{3,2,1,0:T(8,128)S(1)} fusion(f32[32,32,2,64]{3,1,2,0:T(8,128)S(1)} %fusion.7, f32[32,32,2,64]{3,1,2,0:T(8,128)S(1)} %fusion), kind=kOutput, calls=%fused_computation.24 | convolution fusion | flops 100663296 | bytes 2097152 | tf_op jit(solution)/shard_map/btlo,btli->bloi/dot_general | solution.py:37
  25.2 0.7 reshape.39
  25.8 0.0 copy-done.1
  25.8 0.0 copy-done.2
  25.9 0.0 copy-start.4
  25.9 0.0 copy-start.3
  25.9 3.9 %fusion.17 = f32[128,8192]{1,0:T(8,128)} fusion(f32[32,8192]{1,0:T(8,128)S(1)} %reshape.39, s32[32]{0:T(128)S(1)} %bitcast_add_fusion), kind=kOutput, calls=%fused_computation.18 | convolution fusion | flops 402657280 | bytes 5243008 | tf_op jit(solution)/shard_map/dot_general | solution.py:45
  29.8 0.0 all-reduce.4.cloned.1.call-update
  29.8 0.0 copy-done.4
  29.8 0.6 dynamic-slice
  30.4 0.0 copy-done.3
  30.4 0.6 dynamic-slice.2
  32.2 44.6 %all-gather.3.cloned.1.call-done = f32[32,2,8192]{2,1,0:T(2,128)} async-done(((f32[1,2,8192]{2,1,0:T(2,128)}), f32[32,2,8192]{2,1,0:T(2,128)}) %all-gather.3.cloned.1.call-update) | async-done | bytes 2097168 | tf_op jit(solution)/shard_map/all_gather | solution.py:54
  76.7 2.7 reshape.41
  79.4 239.2 %all-reduce.4.cloned.1.call-done = f32[128,8192]{1,0:T(8,128)} async-done(((f32[128,8192]{1,0:T(8,128)}), f32[128,8192]{1,0:T(8,128)}) %all-reduce.4.cloned.1.call-update) | async-done | bytes 4194320
  318.6 2.7 convolution_multiply_fusion
  321.3 24.5 %all-reduce.1 = f32[64,4]{0,1:T(4,128)S(1)} all-reduce(f32[64,4]{0,1:T(4,128)S(1)} %convolution_multiply_fusion), channel_id=3, replica_groups=mesh['ex'=32,'tok'=8] {'tok'}, use_global_device_ids=true, to_apply=%region_1.0.clone | all-reduce | flops 256 | bytes 2048
  345.7 0.7 constant_dynamic-slice_fusion
  (2 shorter events, 0.0 us)
Async XLA Ops:
  6.5 6.5 %copy-start = (bf16[2,1024,64]{1,2,0:T(8,128)(2,1)S(1)}, bf16[2,1024,64]{1,2,0:T(8,128)(2,1)}, u32[]{:S(2)}) copy-start(bf16[2,1024,64]{1,2,0:T(8,128)(2,1)} %param.15) | copy-start | bytes 786436
  6.5 70.2 %all-gather.3.cloned.1.call-start = ((), (), s32[]{:S(2)}) async-start(), calls=%async_computation | async-start | bytes 2162688 | tf_op jit(solution)/shard_map/all_gather | solution.py:54
  10.8 307.8 %all-reduce.4.cloned.1.call-start = ((), (), s32[]{:S(2)}) async-start(), calls=%async_computation.1 | async-start | bytes 8388608
  21.4 4.4 %copy-start.1 = (s32[32]{0:T(128)S(1)}, s32[32]{0:T(128)}, u32[]{:S(2)}) copy-start(s32[32]{0:T(128)} %param.13) | copy-start | bytes 388
  21.4 4.4 %copy-start.2 = (s32[32,1]{0,1:T(1,128)S(1)}, s32[32,1]{0,1:T(1,128)}, u32[]{:S(2)}) copy-start(s32[32,1]{0,1:T(1,128)} %param.12) | copy-start | bytes 388
  25.9 3.9 %copy-start.4 = (u32[256]{0:T(256)S(1)}, u32[256]{0:T(256)}, u32[]{:S(2)}) copy-start(u32[256]{0:T(256)} %constant.12) | copy-start | bytes 3076
  25.9 4.5 %copy-start.3 = (u32[256]{0:T(256)S(1)}, u32[256]{0:T(256)}, u32[]{:S(2)}) copy-start(u32[256]{0:T(256)} %constant.16) | copy-start | bytes 3076
Sparse Core Ops, SparseCore 0:
  10.9 65.7 all-gather.2
  79.4 239.1 all-reduce.3
where the time goes:
time: 354 us; the launch traced here: 353 us
  waiting for transfers between devices  284 us (80%)
  blocking collectives  24.5 us (7%)
  matrix products  21.1 us (6%)
  between operations  14.7 us (4%)
  local copies, waits for them, and re-layouts  8.42 us (2%)
    unnamed x3, waiting for transfers between devices  239 us
    all_gather x1, waiting for transfers between devices, on_device(): lax.all_gather(conditioned, 'ex', axis=0, tiled=True)  44.6 us
    unnamed x1, blocking collectives  24.5 us
  transfers between devices with their start and end apart: 2, of which 2 were waited for; matrix products, arithmetic and copies ran while one was open for 6% of the time, Pallas kernels for 0%

commit v1 on v0

--- a/solution.py
+++ b/solution.py
@@ -8,6 +8,11 @@
 EX_DEV = 4
 F = 8192
 highest = lax.Precision.HIGHEST
+
+
+def exchange_gather(shard, mesh_axis, along):
+    repeated = jnp.stack([shard] * lax.axis_size(mesh_axis))
+    return jnp.concatenate(lax.all_to_all(repeated, mesh_axis, 0, 0), axis=along)
 
 
 def on_device(
@@ -50,9 +55,9 @@
     conditioned = jnp.einsum("qlac,lcd->qlad", left_side, precond[:, 1], precision=highest).reshape(
         query_count, F
     )
-    score_terms = jnp.dot(
-        lax.all_gather(conditioned, "ex", axis=0, tiled=True), features.T, precision=highest
-    ) * (1.0 / (R * BLK))
+    score_terms = jnp.dot(exchange_gather(conditioned, "ex", 0), features.T, precision=highest) * (
+        1.0 / (R * BLK)
+    )
     return lax.psum_scatter(score_terms, "tok", scatter_dimension=0, tiled=True)
 
 

time: 354 us -> 316 us (0.89)
  waiting for transfers between devices: 284 us -> 240 us
  starting transfers between devices: 0.04 us -> 8.35 us
    all_to_all x0 -> x1, waiting for transfers between devices: none -> 50 us  [exchange_gather(): lax.all_to_all(repeated, mesh_axis, 0, 0)]
    unnamed x3 -> x2, waiting for transfers between devices: 239 us -> 190 us
    all_gather x1 -> x0, waiting for transfers between devices: 44.6 us -> none  [on_device(): lax.all_gather(conditioned, 'ex', axis=0, tiled=True)]
    all_to_all x0 -> x1, starting transfers between devices: none -> 8.35 us  [exchange_gather(): lax.all_to_all(repeated, mesh_axis, 0, 0)]
  transfers between devices with their start and end apart: 2 -> 2, of which waited for: 2 -> 2; matrix products, arithmetic and copies ran while one was open for 6% -> 2% of each run, Pallas kernels for 0% -> 0%
where the time goes in v1:
time: 316 us
  waiting for transfers between devices  240 us (76%)
  blocking collectives  24.5 us (8%)
  matrix products  18 us (6%)
  between operations  14.9 us (5%)
  local copies, waits for them, and re-layouts  9.09 us (3%)
  starting transfers between devices  8.35 us (3%)
    unnamed x2, waiting for transfers between devices  190 us
    all_to_all x1, waiting for transfers between devices, exchange_gather(): lax.all_to_all(repeated, mesh_axis, 0, 0)  50 us
    unnamed x1, blocking collectives  24.5 us
    all_to_all x1, starting transfers between devices, exchange_gather(): lax.all_to_all(repeated, mesh_axis, 0, 0)  8.35 us
  transfers between devices with their start and end apart: 2, of which 2 were waited for; matrix products, arithmetic and copies ran while one was open for 2% of the time, Pallas kernels for 0%

profile of v1, /device:TPU:0, one launch (start us, length us, event | category | flops | bytes accessed | tf_op | source)
XLA Modules:
  0.0 315.6 jit_solution(13139260914456991955)
XLA Ops:
  6.5 0.0 copy-start
  6.5 0.0 all-reduce.4.cloned.1.call-start
  6.5 1.5 copy.20
  8.1 0.7 fusion.18
  8.8 0.0 copy-start.3
  8.8 5.0 %fusion = f32[32,32,2,64]{3,1,2,0:T(8,128)S(1)} fusion(bf16[2,64,4096,1]{2,1,0,3:T(8,128)(2,1)S(1)} %bitcast.51, bf16[32,32,4096]{2,1,0:T(8,128)(2,1)} %param.9), kind=kOutput, calls=%fused_computation | convolution fusion | flops 1073741824 | bytes 9961472 | tf_op jit(solution)/shard_map/dot_general | solution.py:32
  13.8 0.0 copy-done
  13.8 0.0 copy-done.3
  13.8 1.2 fusion.7
  15.1 0.0 copy-start.4
  15.1 0.0 copy-start.5
  15.1 3.7 %fusion.21 = f32[32,2,64,64]{3,2,1,0:T(8,128)S(1)} fusion(f32[32,32,2,64]{3,1,2,0:T(8,128)S(1)} %fusion.7, f32[32,32,2,64]{3,1,2,0:T(8,128)S(1)} %fusion), kind=kOutput, calls=%fused_computation.24 | convolution fusion | flops 100663296 | bytes 2097152 | tf_op jit(solution)/shard_map/btlo,btli->bloi/dot_general | solution.py:42
  18.9 0.7 reshape.41
  19.5 0.0 copy-done.4
  19.5 0.0 copy-done.5
  19.5 0.0 copy-start.2
  19.6 0.0 copy-start.1
  19.6 3.9 %fusion.17 = f32[128,8192]{1,0:T(8,128)} fusion(f32[32,8192]{1,0:T(8,128)S(1)} %reshape.41, s32[32]{0:T(128)S(1)} %bitcast_add_fusion), kind=kOutput, calls=%fused_computation.18 | convolution fusion | flops 402657280 | bytes 5243008 | tf_op jit(solution)/shard_map/dot_general | solution.py:50
  23.5 0.0 all-reduce.4.cloned.1.call-update
  23.5 0.0 copy-done.2
  23.5 0.0 copy-start.7
  23.5 0.0 copy-start.6
  23.5 0.1 reshape.39
  23.7 0.0 copy-done.1
  23.7 0.4 convolution_bitcast_fusion.1
  24.1 0.4 convolution_bitcast_fusion
  24.5 0.1 stack_reshape.2
  24.6 2.3 stack.3
  26.9 8.3 %all-to-all-start = ((f32[32,2,8192]{2,1,0:T(2,128)}), f32[32,2,8192]{2,1,0:T(2,128)S(1)}, u32[]{:S(2)}, u32[]{:S(2)}) async-start(f32[32,2,8192]{2,1,0:T(2,128)} %stack.3), calls=%async_computation | async-start | bytes 4194304 | tf_op jit(solution)/shard_map/all_to_all | solution.py:15
  35.2 0.0 copy-done.7
  35.2 0.6 dynamic-slice
  35.8 0.0 copy-done.6
  35.8 0.7 dynamic-slice.2
  37.8 50.0 %all-to-all-done = f32[32,2,8192]{2,1,0:T(2,128)S(1)} async-done(((f32[32,2,8192]{2,1,0:T(2,128)}), f32[32,2,8192]{2,1,0:T(2,128)S(1)}, u32[]{:S(2)}, u32[]{:S(2)}) %all-to-all-start) | async-done | bytes 2097184 | tf_op jit(solution)/shard_map/all_to_all | solution.py:15
  87.8 2.4 reshape.40
  90.2 190.1 %all-reduce.4.cloned.1.call-done = f32[128,8192]{1,0:T(8,128)} async-done(((f32[128,8192]{1,0:T(8,128)}), f32[128,8192]{1,0:T(8,128)}) %all-reduce.4.cloned.1.call-update) | async-done | bytes 4194320
  280.4 3.3 %convolution_multiply_fusion = f32[64,4]{0,1:T(4,128)S(1)} fusion(f32[64,8192]{1,0:T(8,128)} %reshape.40, f32[128,8192]{1,0:T(8,128)} %all-reduce.4.cloned.1.call-done, u32[]{:T(128)S(6)} %multiply.1), kind=kOutput, calls=%fused_computation.8 | convolution fusion | flops 25166080 | bytes 2229252 | tf_op jit(solution)/shard_map/dot_general | solution.py:58
  283.7 24.5 %all-reduce.1 = f32[64,4]{0,1:T(4,128)S(1)} all-reduce(f32[64,4]{0,1:T(4,128)S(1)} %convolution_multiply_fusion), channel_id=3, replica_groups=mesh['ex'=32,'tok'=8] {'tok'}, use_global_device_ids=true, to_apply=%region_1.0.clone | all-reduce | flops 256 | bytes 2048
  308.1 0.7 constant_dynamic-slice_fusion
  (2 shorter events, 0.0 us)
Async XLA Ops:
  6.5 7.3 %copy-start = (bf16[2,1024,64]{1,2,0:T(8,128)(2,1)S(1)}, bf16[2,1024,64]{1,2,0:T(8,128)(2,1)}, u32[]{:S(2)}) copy-start(bf16[2,1024,64]{1,2,0:T(8,128)(2,1)} %param.15) | copy-start | bytes 786436
  6.5 273.8 %all-reduce.4.cloned.1.call-start = ((), (), s32[]{:S(2)}) async-start(), calls=%async_computation.1 | async-start | bytes 8388608
  8.8 5.0 %copy-start.3 = (bf16[32,32,2,1024]{3,2,1,0:T(2,128)(2,1)S(1)}, bf16[32,32,2,1024]{3,2,1,0:T(2,128)(2,1)}, u32[]{:S(2)}) copy-start(bf16[32,32,2,1024]{3,2,1,0:T(2,128)(2,1)} %param.10) | copy-start | bytes 12582916
  15.1 4.4 %copy-start.4 = (s32[32]{0:T(128)S(1)}, s32[32]{0:T(128)}, u32[]{:S(2)}) copy-start(s32[32]{0:T(128)} %param.13) | copy-start | bytes 388
  15.1 4.4 %copy-start.5 = (s32[32,1]{0,1:T(1,128)S(1)}, s32[32,1]{0,1:T(1,128)}, u32[]{:S(2)}) copy-start(s32[32,1]{0,1:T(1,128)} %param.12) | copy-start | bytes 388
  19.5 3.9 %copy-start.2 = (f32[2,8192]{1,0:T(2,128)S(1)}, f32[2,8192]{1,0:T(2,128)}, u32[]{:S(2)}) copy-start(f32[2,8192]{1,0:T(2,128)} %param.16) | copy-start | bytes 196612
  19.6 4.1 %copy-start.1 = (f32[2,2,64,64]{3,2,1,0:T(8,128)S(1)}, f32[2,2,64,64]{3,2,1,0:T(8,128)}, u32[]{:S(2)}) copy-start(f32[2,2,64,64]{3,2,1,0:T(8,128)} %param.17) | copy-start | bytes 196612
  23.5 11.7 %copy-start.7 = (u32[256]{0:T(256)S(1)}, u32[256]{0:T(256)}, u32[]{:S(2)}) copy-start(u32[256]{0:T(256)} %constant.12) | copy-start | bytes 3076
  23.5 12.3 %copy-start.6 = (u32[256]{0:T(256)S(1)}, u32[256]{0:T(256)}, u32[]{:S(2)}) copy-start(u32[256]{0:T(256)} %constant.16) | copy-start | bytes 3076
  26.9 60.9 %all-to-all-start = ((f32[32,2,8192]{2,1,0:T(2,128)}), f32[32,2,8192]{2,1,0:T(2,128)S(1)}, u32[]{:S(2)}, u32[]{:S(2)}) async-start(f32[32,2,8192]{2,1,0:T(2,128)} %stack.3), calls=%async_computation | async-start | bytes 4194304 | tf_op jit(solution)/shard_map/all_to_all | solution.py:15
Sparse Core Ops, SparseCore 0:
  23.6 256.7 all-reduce.3
